TPU v7x, 32 devices: a whole 2x2x4 slice. The times are simulated.
32 devices in a mesh: lon: 16 (over z, y, x), lev: 2 (over core).
Axes of the slice: x: 2, y: 2, z: 4, core: 2. Of those that a mesh axis runs over, the one named last changes fastest.
Arguments:
- ensemble: float32 [80, 16, 16384], P(None, 'lev', 'lon'), may hold values from -6 to 6
- obs_cell: int32 [12, 128], P(None, 'lon'), may hold values from 0 to 16383, as said below
- obs_value: float32 [12, 128], P(None, 'lon'), may hold values from -5 to 5
- obs_noise: float32 [12, 128], P(None, 'lon'), may hold values from 0.2 to 2
- obs_weight: float32 [12, 16, 128], P(None, 'lev'), may hold values from 0.05 to 0.5
- tile_lists: int32 [12, 384], P(None, 'lon'), may hold values from 0 to 128, as said below
- batch_order: int32 [12], replicated, may hold values from 0 to 11, each once
Outputs:
- analysis: float32 [80, 16, 16384], P(None, 'lev', 'lon')
Inputs may be any that keep to these rules, and one draw needn't show every extreme that they name: `obs_cell`: each tile holds at most 8 observations of one block, and some tile exactly 8. `tile_lists`: for block b and tile t the tile's 24 slots hold first, ascending and once each, the observations of block b whose tile is t or a neighbour of t around the globe, then the value 128 in every remaining slot; in every block some tile has all 24 slots used. `batch_order`: each block once.
All inputs are finite; a program needn't handle non-finite values.
Results may differ from a plain program's by a relative error of at most 0.0003.
Values sent between devices are 32-bit elements; how exact they have to be, the bound alone decides.
A program may use at most 128 MiB of HBM per device.

v0:
```python
import jax
import jax.numpy as jnp
from jax import lax
from jax.sharding import PartitionSpec as P

MEM = 80
OBS = 128
ROUTE_CAP = 24
LON_DEV = 16
CELL_DEV = 1024
BATCHES = 12


highest = lax.Precision.HIGHEST


def locate(cell_ids):
    within = cell_ids % CELL_DEV
    return (within // LON_DEV, cell_ids // CELL_DEV * LON_DEV + within % LON_DEV)


def taper_weight(source_ids, target_ids, circle):
    source_row, source_col = locate(source_ids)
    target_row, target_col = locate(target_ids)
    apart_cols = jnp.abs(source_col[:, None] - target_col[None, :])
    apart_cols = jnp.minimum(apart_cols, circle - apart_cols)
    apart_rows = source_row[:, None] - target_row[None, :]
    square = (apart_cols * apart_cols + apart_rows * apart_rows).astype(jnp.float32)
    return jnp.exp(square * (-2.0 / (LON_DEV * LON_DEV)))


def gain_parts(sample_now, observed, noise):
    centre = jnp.mean(sample_now, axis=0)
    spread = sample_now - centre
    covariance = jnp.dot(spread.T, spread, precision=highest) / (MEM - 1) + jnp.diag(noise)
    factor = jnp.linalg.cholesky(covariance)
    innovation = (observed - centre)[:, None]
    halfway = lax.linalg.triangular_solve(factor, innovation, left_side=True, lower=True)
    kalman_gain = lax.linalg.triangular_solve(
        factor, halfway, left_side=True, lower=True, transpose_a=True
    )[:, 0]
    rooted = factor + jnp.diag(jnp.sqrt(noise))
    identity = jnp.eye(OBS, dtype=noise.dtype)
    within = lax.linalg.triangular_solve(rooted, identity, left_side=True, lower=True)
    reduced = lax.linalg.triangular_solve(
        factor, within, left_side=True, lower=True, transpose_a=True
    )
    return (spread, kalman_gain, reduced)


def update_block(block, spread, kalman_gain, reduced, chosen, usable, obs_ids, local_ids, circle):
    levels = block.shape[1]
    rows_used = chosen.shape[0]
    weight = taper_weight(obs_ids[chosen], local_ids, circle) * usable[:, None]
    centre = jnp.mean(block, axis=0)
    flattened = (block - centre).reshape(MEM, -1)
    crossed = jnp.dot(spread[:, chosen].T, flattened, precision=highest) / (MEM - 1)
    tapered = (crossed.reshape(rows_used, levels, -1) * weight[:, None, :]).reshape(rows_used, -1)
    shifted = jnp.dot(kalman_gain[chosen], tapered, precision=highest)
    mixing = jnp.dot(spread, reduced[chosen].T, precision=highest)
    flattened = flattened - jnp.dot(mixing, tapered, precision=highest)
    return ((centre.reshape(-1) + shifted)[None, :] + flattened).reshape(block.shape)


def correct(upcoming, next_ids, now_ids, spread, kalman_gain, reduced, listed, circle, numbers):
    owners = next_ids // CELL_DEV
    lists_rows = listed.reshape(-1, ROUTE_CAP)[owners]
    member = jnp.any(lists_rows[:, :, None] == numbers[None, None, :], axis=1)
    weight = taper_weight(now_ids, next_ids, circle) * member.T.astype(jnp.float32)
    centre = jnp.mean(upcoming, axis=0)
    departure = upcoming - centre
    crossed = jnp.dot(spread.T, departure, precision=highest) / (MEM - 1)
    tapered = crossed * weight
    shifted = jnp.dot(kalman_gain, tapered, precision=highest)
    mixing = jnp.dot(spread, reduced.T, precision=highest)
    return (centre + shifted)[None, :] + departure - jnp.dot(mixing, tapered, precision=highest)


def body(ensemble, obs_cell, obs_value, obs_noise, obs_weight, tile_lists, batch_order):
    cell_table = lax.all_gather(obs_cell, "lon", axis=1, tiled=True)
    observed, noise = (
        lax.all_gather(obs_value, "lon", axis=1, tiled=True),
        lax.all_gather(obs_noise, "lon", axis=1, tiled=True),
    )
    tile_index = lax.axis_index("lon")
    circle = LON_DEV * lax.axis_size("lon")
    offset = tile_index * CELL_DEV
    local_ids = offset + jnp.arange(CELL_DEV, dtype=jnp.int32)
    numbers = jnp.arange(OBS, dtype=jnp.int32)

    def portion_of(block, current):
        cell_ids = cell_table[current]
        owned = ((cell_ids >= offset) & (cell_ids < offset + CELL_DEV)).astype(jnp.float32)
        within = jnp.clip(cell_ids - offset, 0, CELL_DEV - 1)
        picked = jnp.take(block, within, axis=2)
        return jnp.sum(picked * (obs_weight[current] * owned[None, :])[None], axis=1)

    def advance(block, sample_now, current):
        spread, kalman_gain, reduced = gain_parts(sample_now, observed[current], noise[current])
        listed = tile_lists[current]
        usable = jnp.any(listed[:, None] == numbers[None, :], axis=0).astype(jnp.float32)
        block = update_block(
            block,
            spread,
            kalman_gain,
            reduced,
            numbers,
            usable,
            cell_table[current],
            local_ids,
            circle,
        )
        return (block, spread, kalman_gain, reduced)

    every_lists = lax.all_gather(tile_lists, "lon", axis=1, tiled=True)
    block_ids = jnp.arange(BATCHES, dtype=jnp.int32)
    portions = jax.vmap(lambda which: portion_of(ensemble, which))(block_ids)
    probes = lax.psum(portions, ("lon", "lev"))

    def serial_turn(position, carried):
        block, probes = carried
        current = batch_order[position]
        block, spread, kalman_gain, reduced = advance(block, probes[current], current)

        def renew(upcoming, next_ids):
            return correct(
                upcoming,
                next_ids,
                cell_table[current],
                spread,
                kalman_gain,
                reduced,
                every_lists[current],
                circle,
                numbers,
            )

        probes = jax.vmap(renew)(probes, cell_table)
        return (block, probes)

    carried = (ensemble, probes)

    def grouped(groups, carried):
        for repeat in range(4):
            carried = serial_turn(4 * groups + repeat, carried)
        return carried

    finished = lax.fori_loop(0, BATCHES // 4, grouped, carried)
    return finished[0]


def solution(mesh):
    return jax.shard_map(
        body,
        mesh=mesh,
        in_specs=(
            P(None, "lev", "lon"),
            P(None, "lon"),
            P(None, "lon"),
            P(None, "lon"),
            P(None, "lev", None),
            P(None, "lon"),
            P(),
        ),
        out_specs=P(None, "lev", "lon"),
        check_vma=False,
    )
```

profile of v0, /device:TPU:29, one launch (start us, length us, event | category | flops | bytes accessed | tf_op | source)
XLA Modules:
  0.0 1285.2 jit_solution(17468033664224430535)
XLA Ops:
  8.3 27.4 %all_gather.12 = s32[12,128]{0,1:T(8,128)S(1)} all-gather(s32[12,8]{0,1:T(8,128)S(1)} %copy-done.59), channel_id=1, replica_groups=mesh['lon'=16,'lev'=2] {'lon'}, dimensions={1}, use_global_device_ids=true | all-gather | bytes 6528 | tf_op jit(solution)/shard_map/all_gather | solution.py:80
  54.2 31.7 %all-gather = s32[16,24,12]{1,2,0:T(8,128)S(1)} all-gather(s32[1,24,12]{1,2,0:T(8,128)S(1)} %bitcast.782), channel_id=1, replica_groups=mesh['lon'=16,'lev'=2] {'lon'}, dimensions={0}, use_global_device_ids=true | all-gather | bytes 19584 | tf_op jit(solution)/shard_map/all_gather | solution.py:115
  86.0 29.1 %all_gather.13 = f32[12,128]{0,1:T(8,128)S(1)} all-gather(f32[12,8]{0,1:T(8,128)S(1)} %copy-done.60), channel_id=1, replica_groups=mesh['lon'=16,'lev'=2] {'lon'}, dimensions={1}, use_global_device_ids=true | all-gather | bytes 6528 | tf_op jit(solution)/shard_map/all_gather | solution.py:83
  115.2 30.7 %all_gather.14 = f32[12,128]{0,1:T(8,128)S(1)} all-gather(f32[12,8]{0,1:T(8,128)S(1)} %copy-done.61), channel_id=1, replica_groups=mesh['lon'=16,'lev'=2] {'lon'}, dimensions={1}, use_global_device_ids=true | all-gather | bytes 6528 | tf_op jit(solution)/shard_map/all_gather | solution.py:82
  146.0 44.6 %all-reduce.2.cloned.1.call-done = f32[12,80,128]{1,2,0:T(8,128)} async-done(((f32[12,80,128]{1,2,0:T(8,128)}), f32[12,80,128]{1,2,0:T(8,128)}) %all-reduce.2.cloned.1.call-update) | async-done | bytes 491536 | tf_op jit(solution)/shard_map/psum | solution.py:118
  194.2 1081.6 %while.22 = (s32[]{:T(128)}, f32[80,8,1024]{2,1,0:T(8,128)S(1)}, f32[12,80,128]{2,1,0:T(8,128)}, s32[12]{0:T(128)S(1)}, f32[12,128]{1,0:T(8,128)S(1)}, /*index=5...) while((s32[]{:T(128)}, f32[80,8,1024]{2,1,0:T(8,128)S(1)}, ...), condition=%wide.region_25.31_spmd.clone.clone.clone, body=%wide.region_2.30_spmd.clone.clone.clone.sunk | while | flops 10092335104 | bytes 268165232 | solution.py:148
  223.7 11.7 cholesky.398
  236.7 9.8 custom-call.137
  248.6 9.8 custom-call.136
  262.3 12.3 cholesky.399
  293.3 10.4 fusion.631
  311.3 10.7 custom-call.138
  327.3 11.7 cholesky.400
  341.0 9.8 custom-call.141
  356.6 10.6 fusion.641
  372.4 9.8 custom-call.140
  389.8 10.4 fusion.678
  406.7 11.7 cholesky.401
  419.9 9.8 custom-call.143
  431.7 9.8 custom-call.142
  584.1 11.7 cholesky.398
  597.1 9.8 custom-call.137
  609.0 9.8 custom-call.136
  622.6 11.9 cholesky.399
  653.3 10.4 fusion.631
  671.3 10.7 custom-call.138
  687.3 11.7 cholesky.400
  701.0 9.8 custom-call.141
  716.6 10.8 fusion.641
  732.6 9.8 custom-call.140
  750.0 10.4 fusion.678
  766.7 11.7 cholesky.401
  779.8 9.8 custom-call.143
  791.7 9.8 custom-call.142
  944.1 11.7 cholesky.398
  957.1 9.8 custom-call.137
  969.0 9.8 custom-call.136
  982.7 11.9 cholesky.399
  1013.4 10.4 fusion.631
  1031.6 10.7 custom-call.138
  1047.6 11.7 cholesky.400
  1061.3 9.8 custom-call.141
  1076.9 10.6 fusion.641
  1092.7 9.8 custom-call.140
  1110.0 10.4 fusion.678
  1126.8 11.7 cholesky.401
  1139.9 9.8 custom-call.143
  1151.8 9.8 custom-call.142
  (898 shorter events, 635.1 us)
Async XLA Ops:
  6.5 29.9 %copy-start = (f32[12,8,128]{2,1,0:T(8,128)S(1)}, f32[12,8,128]{2,1,0:T(8,128)}, u32[]{:S(2)}) copy-start(f32[12,8,128]{2,1,0:T(8,128)} %param.22) | copy-start | bytes 147460
  6.5 184.0 %all-reduce.2.cloned.1.call-start = ((), (), s32[]{:S(2)}) async-start(), calls=%async_computation | async-start | bytes 1572864 | tf_op jit(solution)/shard_map/psum | solution.py:118
  47.4 38.6 %copy-start.60 = (f32[12,8]{0,1:T(8,128)S(1)}, f32[12,8]{0,1:T(8,128)}, u32[]{:S(2)}) copy-start(f32[12,8]{0,1:T(8,128)} %param.21) | copy-start | bytes 1156
  47.4 67.8 %copy-start.61 = (f32[12,8]{0,1:T(8,128)S(1)}, f32[12,8]{0,1:T(8,128)}, u32[]{:S(2)}) copy-start(f32[12,8]{0,1:T(8,128)} %param.20) | copy-start | bytes 1156
  47.4 146.7 %copy-start.32 = (s32[12]{0:T(128)S(1)}, s32[12]{0:T(128)}, u32[]{:S(2)}) copy-start(s32[12]{0:T(128)} %param.24) | copy-start | bytes 148
  194.5 25.5 %copy-start.15 = (s32[12,128]{1,0:T(8,128)}, s32[12,128]{1,0:T(8,128)S(1)}, u32[]{:S(2)}) copy-start(s32[12,128]{1,0:T(8,128)S(1)} %get-tuple-element.1329) | copy-start | bytes 18436 | tf_op jit(solution)/shard_map/while
  194.5 25.5 %copy-start.26 = (s32[12,1,128]{2,0,1:T(8,128)}, s32[12,1,128]{2,0,1:T(8,128)S(1)}, u32[]{:S(2)}) copy-start(s32[12,1,128]{2,0,1:T(8,128)S(1)} %get-tuple-element.1334) | copy-start | bytes 18436 | tf_op jit(solution)/shard_map/while
  194.5 25.5 %copy-start.28 = (s32[12,1,128]{2,0,1:T(8,128)}, s32[12,1,128]{2,0,1:T(8,128)S(1)}, u32[]{:S(2)}) copy-start(s32[12,1,128]{2,0,1:T(8,128)S(1)} %get-tuple-element.1335) | copy-start | bytes 18436 | tf_op jit(solution)/shard_map/while
  194.5 25.5 %copy-start.30 = (s32[12,128]{1,0:T(8,128)}, s32[12,128]{1,0:T(8,128)S(1)}, u32[]{:S(2)}) copy-start(s32[12,128]{1,0:T(8,128)S(1)} %get-tuple-element.1336) | copy-start | bytes 18436 | tf_op jit(solution)/shard_map/while
  194.5 52.0 %copy-start.50 = (f32[12,128]{1,0:T(8,128)}, f32[12,128]{1,0:T(8,128)S(1)}, u32[]{:S(2)}) copy-start(f32[12,128]{1,0:T(8,128)S(1)} %get-tuple-element.1328) | copy-start | bytes 18436 | tf_op jit(solution)/shard_map/while
  216.1 238.8 %copy-start.18 = (s32[1024]{0:T(1024)}, s32[1024]{0:T(1024)S(1)}, u32[]{:S(2)}) copy-start(s32[1024]{0:T(1024)S(1)} %pad_clamp_fusion.6) | copy-start | bytes 12292 | tf_op jit(solution)/shard_map/while
  220.1 26.7 %copy-start.34 = (s32[12,128]{1,0:T(8,128)}, s32[12,128]{1,0:T(8,128)S(1)}, u32[]{:S(2)}) copy-start(s32[12,128]{1,0:T(8,128)S(1)} %get-tuple-element.1189) | copy-start | bytes 18436 | tf_op jit(solution)/shard_map/while
  220.1 26.5 %copy-start.20 = (f32[12,128]{1,0:T(8,128)}, f32[12,128]{1,0:T(8,128)S(1)}, u32[]{:S(2)}) copy-start(f32[12,128]{1,0:T(8,128)S(1)} %broadcast_multiply_fusion.27) | copy-start | bytes 18436 | tf_op jit(solution)/shard_map/while
  293.3 30.3 %copy-start.21 = (f32[12,128]{1,0:T(8,128)S(1)}, f32[12,128]{1,0:T(8,128)}, u32[]{:S(2)}) copy-start(f32[12,128]{1,0:T(8,128)} %broadcast_multiply_fusion.29) | copy-start | bytes 18436 | tf_op jit(solution)/shard_map/while
  356.6 29.4 %copy-start.38 = (s32[384]{0:T(512)S(1)}, s32[384]{0:T(512)}, u32[]{:S(2)}) copy-start(s32[384]{0:T(512)} %get-tuple-element.1265) | copy-start | bytes 4612 | tf_op jit(solution)/shard_map/while
  389.8 29.4 %copy-start.41 = (f32[128]{0:T(128)S(1)}, f32[128]{0:T(128)}, u32[]{:S(2)}) copy-start(f32[128]{0:T(128)} %get-tuple-element.1227) | copy-start | bytes 1540 | tf_op jit(solution)/shard_map/while
  389.8 39.9 %copy-start.51 = (f32[12,128]{1,0:T(8,128)S(1)}, f32[12,128]{1,0:T(8,128)}, u32[]{:S(2)}) copy-start(f32[12,128]{1,0:T(8,128)} %copy-done.50) | copy-start | bytes 18436 | tf_op jit(solution)/shard_map/while
  400.2 46.4 %copy-start.42 = (s32[128]{0:T(128)S(1)}, s32[128]{0:T(128)}, u32[]{:S(2)}) copy-start(s32[128]{0:T(128)} %get-tuple-element.1236) | copy-start | bytes 1540 | tf_op jit(solution)/shard_map/while
  400.2 46.4 %copy-start.43 = (s32[128]{0:T(128)S(1)}, s32[128]{0:T(128)}, u32[]{:S(2)}) copy-start(s32[128]{0:T(128)} %get-tuple-element.1234) | copy-start | bytes 1540 | tf_op jit(solution)/shard_map/while
  400.2 46.4 %copy-start.44 = (s32[128]{0:T(128)S(1)}, s32[128]{0:T(128)}, u32[]{:S(2)}) copy-start(s32[128]{0:T(128)} %get-tuple-element.1239) | copy-start | bytes 1540 | tf_op jit(solution)/shard_map/while
  400.2 46.4 %copy-start.45 = (s32[128]{0:T(128)S(1)}, s32[128]{0:T(128)}, u32[]{:S(2)}) copy-start(s32[128]{0:T(128)} %get-tuple-element.1238) | copy-start | bytes 1540 | tf_op jit(solution)/shard_map/while
  554.8 25.5 %copy-start.15 = (s32[12,128]{1,0:T(8,128)}, s32[12,128]{1,0:T(8,128)S(1)}, u32[]{:S(2)}) copy-start(s32[12,128]{1,0:T(8,128)S(1)} %get-tuple-element.1329) | copy-start | bytes 18436 | tf_op jit(solution)/shard_map/while
  554.9 25.5 %copy-start.26 = (s32[12,1,128]{2,0,1:T(8,128)}, s32[12,1,128]{2,0,1:T(8,128)S(1)}, u32[]{:S(2)}) copy-start(s32[12,1,128]{2,0,1:T(8,128)S(1)} %get-tuple-element.1334) | copy-start | bytes 18436 | tf_op jit(solution)/shard_map/while
  554.9 25.5 %copy-start.28 = (s32[12,1,128]{2,0,1:T(8,128)}, s32[12,1,128]{2,0,1:T(8,128)S(1)}, u32[]{:S(2)}) copy-start(s32[12,1,128]{2,0,1:T(8,128)S(1)} %get-tuple-element.1335) | copy-start | bytes 18436 | tf_op jit(solution)/shard_map/while
  554.9 52.0 %copy-start.50 = (f32[12,128]{1,0:T(8,128)}, f32[12,128]{1,0:T(8,128)S(1)}, u32[]{:S(2)}) copy-start(f32[12,128]{1,0:T(8,128)S(1)} %get-tuple-element.1328) | copy-start | bytes 18436 | tf_op jit(solution)/shard_map/while
  576.5 238.5 %copy-start.18 = (s32[1024]{0:T(1024)}, s32[1024]{0:T(1024)S(1)}, u32[]{:S(2)}) copy-start(s32[1024]{0:T(1024)S(1)} %pad_clamp_fusion.6) | copy-start | bytes 12292 | tf_op jit(solution)/shard_map/while
  580.4 26.7 %copy-start.34 = (s32[12,128]{1,0:T(8,128)}, s32[12,128]{1,0:T(8,128)S(1)}, u32[]{:S(2)}) copy-start(s32[12,128]{1,0:T(8,128)S(1)} %get-tuple-element.1189) | copy-start | bytes 18436 | tf_op jit(solution)/shard_map/while
  580.4 26.5 %copy-start.20 = (f32[12,128]{1,0:T(8,128)}, f32[12,128]{1,0:T(8,128)S(1)}, u32[]{:S(2)}) copy-start(f32[12,128]{1,0:T(8,128)S(1)} %broadcast_multiply_fusion.27) | copy-start | bytes 18436 | tf_op jit(solution)/shard_map/while
  653.3 30.3 %copy-start.21 = (f32[12,128]{1,0:T(8,128)S(1)}, f32[12,128]{1,0:T(8,128)}, u32[]{:S(2)}) copy-start(f32[12,128]{1,0:T(8,128)} %broadcast_multiply_fusion.29) | copy-start | bytes 18436 | tf_op jit(solution)/shard_map/while
  716.6 29.6 %copy-start.38 = (s32[384]{0:T(512)S(1)}, s32[384]{0:T(512)}, u32[]{:S(2)}) copy-start(s32[384]{0:T(512)} %get-tuple-element.1265) | copy-start | bytes 4612 | tf_op jit(solution)/shard_map/while
  750.0 29.1 %copy-start.41 = (f32[128]{0:T(128)S(1)}, f32[128]{0:T(128)}, u32[]{:S(2)}) copy-start(f32[128]{0:T(128)} %get-tuple-element.1227) | copy-start | bytes 1540 | tf_op jit(solution)/shard_map/while
  750.0 39.7 %copy-start.51 = (f32[12,128]{1,0:T(8,128)S(1)}, f32[12,128]{1,0:T(8,128)}, u32[]{:S(2)}) copy-start(f32[12,128]{1,0:T(8,128)} %copy-done.50) | copy-start | bytes 18436 | tf_op jit(solution)/shard_map/while
  760.4 46.2 %copy-start.42 = (s32[128]{0:T(128)S(1)}, s32[128]{0:T(128)}, u32[]{:S(2)}) copy-start(s32[128]{0:T(128)} %get-tuple-element.1236) | copy-start | bytes 1540 | tf_op jit(solution)/shard_map/while
  760.4 46.2 %copy-start.43 = (s32[128]{0:T(128)S(1)}, s32[128]{0:T(128)}, u32[]{:S(2)}) copy-start(s32[128]{0:T(128)} %get-tuple-element.1234) | copy-start | bytes 1540 | tf_op jit(solution)/shard_map/while
  760.4 46.2 %copy-start.44 = (s32[128]{0:T(128)S(1)}, s32[128]{0:T(128)}, u32[]{:S(2)}) copy-start(s32[128]{0:T(128)} %get-tuple-element.1239) | copy-start | bytes 1540 | tf_op jit(solution)/shard_map/while
  760.5 46.2 %copy-start.45 = (s32[128]{0:T(128)S(1)}, s32[128]{0:T(128)}, u32[]{:S(2)}) copy-start(s32[128]{0:T(128)} %get-tuple-element.1238) | copy-start | bytes 1540 | tf_op jit(solution)/shard_map/while
  914.9 52.0 %copy-start.50 = (f32[12,128]{1,0:T(8,128)}, f32[12,128]{1,0:T(8,128)S(1)}, u32[]{:S(2)}) copy-start(f32[12,128]{1,0:T(8,128)S(1)} %get-tuple-element.1328) | copy-start | bytes 18436 | tf_op jit(solution)/shard_map/while
  936.5 238.7 %copy-start.18 = (s32[1024]{0:T(1024)}, s32[1024]{0:T(1024)S(1)}, u32[]{:S(2)}) copy-start(s32[1024]{0:T(1024)S(1)} %pad_clamp_fusion.6) | copy-start | bytes 12292 | tf_op jit(solution)/shard_map/while
  940.5 26.7 %copy-start.34 = (s32[12,128]{1,0:T(8,128)}, s32[12,128]{1,0:T(8,128)S(1)}, u32[]{:S(2)}) copy-start(s32[12,128]{1,0:T(8,128)S(1)} %get-tuple-element.1189) | copy-start | bytes 18436 | tf_op jit(solution)/shard_map/while
  940.5 26.5 %copy-start.20 = (f32[12,128]{1,0:T(8,128)}, f32[12,128]{1,0:T(8,128)S(1)}, u32[]{:S(2)}) copy-start(f32[12,128]{1,0:T(8,128)S(1)} %broadcast_multiply_fusion.27) | copy-start | bytes 18436 | tf_op jit(solution)/shard_map/while
  1013.4 30.5 %copy-start.21 = (f32[12,128]{1,0:T(8,128)S(1)}, f32[12,128]{1,0:T(8,128)}, u32[]{:S(2)}) copy-start(f32[12,128]{1,0:T(8,128)} %broadcast_multiply_fusion.29) | copy-start | bytes 18436 | tf_op jit(solution)/shard_map/while
  1076.9 29.3 %copy-start.38 = (s32[384]{0:T(512)S(1)}, s32[384]{0:T(512)}, u32[]{:S(2)}) copy-start(s32[384]{0:T(512)} %get-tuple-element.1265) | copy-start | bytes 4612 | tf_op jit(solution)/shard_map/while
  1110.0 29.2 %copy-start.41 = (f32[128]{0:T(128)S(1)}, f32[128]{0:T(128)}, u32[]{:S(2)}) copy-start(f32[128]{0:T(128)} %get-tuple-element.1227) | copy-start | bytes 1540 | tf_op jit(solution)/shard_map/while
  1110.0 39.7 %copy-start.51 = (f32[12,128]{1,0:T(8,128)S(1)}, f32[12,128]{1,0:T(8,128)}, u32[]{:S(2)}) copy-start(f32[12,128]{1,0:T(8,128)} %copy-done.50) | copy-start | bytes 18436 | tf_op jit(solution)/shard_map/while
  1120.4 46.3 %copy-start.42 = (s32[128]{0:T(128)S(1)}, s32[128]{0:T(128)}, u32[]{:S(2)}) copy-start(s32[128]{0:T(128)} %get-tuple-element.1236) | copy-start | bytes 1540 | tf_op jit(solution)/shard_map/while
  1120.5 46.3 %copy-start.43 = (s32[128]{0:T(128)S(1)}, s32[128]{0:T(128)}, u32[]{:S(2)}) copy-start(s32[128]{0:T(128)} %get-tuple-element.1234) | copy-start | bytes 1540 | tf_op jit(solution)/shard_map/while
  1120.5 46.3 %copy-start.44 = (s32[128]{0:T(128)S(1)}, s32[128]{0:T(128)}, u32[]{:S(2)}) copy-start(s32[128]{0:T(128)} %get-tuple-element.1239) | copy-start | bytes 1540 | tf_op jit(solution)/shard_map/while
  1120.5 46.3 %copy-start.45 = (s32[128]{0:T(128)S(1)}, s32[128]{0:T(128)}, u32[]{:S(2)}) copy-start(s32[128]{0:T(128)} %get-tuple-element.1238) | copy-start | bytes 1540 | tf_op jit(solution)/shard_map/while
  (123 other events, 981.6 us)
Sparse Core Ops, SparseCore 0:
  53.9 136.6 all-reduce.1
where the time goes:
time: 1300 us; the launch traced here: 1290 us
  other arithmetic  560 us (43%)
  matrix products  301 us (23%)
  local copies, waits for them, and re-layouts  219 us (17%)
  blocking collectives  119 us (9%)
  waiting for transfers between devices  44.6 us (3%)
  loops' own time  28.4 us (2%)
  between operations  13.8 us (1%)
    another operation x36, other arithmetic, gain_parts(): factor = jnp.linalg.cholesky(covariance)  150 us
    another operation x24, other arithmetic, gain_parts(): lax.linalg.triangular_solve(factor, halfway, left_side=True, lower=True,...  132 us
    reduce_or x12, other arithmetic, correct(): member = jnp.any(lists_rows[:, :, None] == numbers[None, None, :], axis=1)  122 us
    another operation x12, other arithmetic, gain_parts(): lax.linalg.triangular_solve(rooted, identity, left_side=True, lower=True)  120 us
    while x342, local copies, waits for them, and re-layouts  83.3 us
    dot_general x12, matrix products, update_block(): jnp.dot(spread[:, chosen].T, flattened, precision=highest) / (MEM - 1)  76.3 us
    dot_general x12, matrix products, update_block(): flattened = flattened - jnp.dot(mixing, tapered, precision=highest)  69.7 us
    dot_general x12, matrix products, update_block(): shifted = jnp.dot(kalman_gain[chosen], tapered, precision=highest)  51.1 us
  transfers between devices with their start and end apart: 1, of which 1 were waited for; matrix products, arithmetic and copies ran while one was open for 0% of the time, Pallas kernels for 0%

commit v1 on v0

v1 whole, which is shorter than its diff:
```python
import functools

import jax
import jax.numpy as jnp
from jax import lax
from jax.experimental import pallas as pl
from jax.experimental.pallas import tpu as pltpu
from jax.sharding import PartitionSpec as P

LON_DEV = 16
CELL_DEV = 1024
PANEL = 8

highest = lax.Precision.HIGHEST
f32 = jnp.float32
bf16 = jnp.bfloat16


def split(x):
    high = x.astype(bf16)
    low = (x - high.astype(f32)).astype(bf16)
    return high, low


def dot(a, b):
    return jnp.dot(a, b, preferred_element_type=f32)


def tapered_weight(row_a, col_a, row_c, col_c, circle):
    e = jnp.abs(col_a - col_c)
    e = jnp.minimum(e, circle - e)
    d = row_a - row_c
    return jnp.exp((e * e + d * d) * (-2.0 / (LON_DEV * LON_DEV)))


def eliminate(a_ref, b_ref, noise_root, mem, obs, width):
    lane = lax.broadcasted_iota(jnp.int32, (1, obs), 1)
    sample = lax.broadcasted_iota(jnp.int32, (1, width), 1) < mem
    for start in range(0, obs, PANEL):
        spot = [[None] * PANEL for _ in range(PANEL)]
        for i in range(PANEL):
            for s in range(i + 1):
                spot[i][s] = jnp.broadcast_to(
                    a_ref[start + i : start + i + 1, start + s : start + s + 1], (1, obs)
                )
        in_panel = (lane >= start) & (lane < start + PANEL)
        rows = []
        sides = []
        for i in range(PANEL):
            row = a_ref[start + i : start + i + 1, :]
            rows.append(jnp.where(in_panel, jnp.where(lane == start + i, 1.0, 0.0), row))
            sides.append(b_ref[start + i : start + i + 1, :])
        scaled_rows = []
        scaled_sides = []
        for r in range(PANEL):
            pivot = spot[r][r]
            inverse_root = lax.rsqrt(pivot)
            inverse = inverse_root * inverse_root
            root = pivot * inverse_root
            added = jnp.where(sample, noise_root[start + r], 0.0)
            factor = 1.0 / (root + added)
            below = [spot[i][r] * inverse for i in range(r + 1, PANEL)]
            for n, i in enumerate(range(r + 1, PANEL)):
                for s in range(r + 1, i + 1):
                    spot[i][s] = spot[i][s] - below[n] * spot[s][r]
            solved = sides[r] * factor
            passing = solved * root
            for n, i in enumerate(range(r + 1, PANEL)):
                rows[i] = rows[i] - below[n] * rows[r]
                sides[i] = sides[i] - below[n] * passing
            scaled_rows.append(rows[r] * inverse)
            scaled_sides.append(solved * inverse_root)
            a_ref[start + r : start + r + 1, :] = jnp.where(
                lane < start + PANEL, rows[r] * inverse_root, 0.0
            )
            b_ref[start + r : start + r + 1, :] = solved
        after = start + PANEL
        if after < obs:
            upper = jnp.concatenate(rows, axis=0)
            left = upper.T[after:, :]
            right = jnp.concatenate(
                [jnp.concatenate(scaled_rows, axis=0), jnp.concatenate(scaled_sides, axis=0)], axis=1
            )
            change = jnp.dot(left, right, precision=highest, preferred_element_type=f32)
            a_ref[after:, :] = jnp.where(in_panel, 0.0, a_ref[after:, :]) - change[:, :obs]
            b_ref[after:, :] = b_ref[after:, :] - change[:, obs:]


def kernel_body(
    x_ref, probe_ref, value_ref, noise_ref, noise_col_ref, cell_row_ref, cell_col_ref, list_ref,
    out_ref, probes, a_ref, b_ref, *, batches, levels, mem, obs, cells, slots, axis_size,
):
    tile = lax.axis_index("lon")
    circle = float(LON_DEV * axis_size)
    scale = 1.0 / (mem - 1)
    probes[...] = probe_ref[...]
    cell = lax.broadcasted_iota(jnp.int32, (1, cells), 1)
    here_row = (cell // LON_DEV).astype(f32)
    here_col = (tile * LON_DEV + cell % LON_DEV).astype(f32)
    target = cell_row_ref[...]
    target_tile = target // CELL_DEV
    target_within = target - target_tile * CELL_DEV
    target_row_int = target_within // LON_DEV
    target_col = (target_tile * LON_DEV + target_within - target_row_int * LON_DEV).astype(f32)
    target_row = target_row_int.astype(f32)
    target_tile = target_tile.astype(f32)
    lanes = lax.broadcasted_iota(jnp.int32, (obs, obs), 1)
    subs = lax.broadcasted_iota(jnp.int32, (obs, obs), 0)

    def turn(k, carry):
        now = probes[k]
        centre = jnp.mean(now, axis=0, keepdims=True)
        spread = now - centre
        innovation = value_ref[k] - centre
        padded = jnp.concatenate(
            [spread, innovation, jnp.zeros((obs - mem - 1, obs), f32)], axis=0
        )
        sides = padded.T
        noise_row = noise_ref[k]
        covariance = jnp.dot(sides[:, :mem], spread, precision=highest, preferred_element_type=f32) * scale
        a_ref[...] = covariance + jnp.where(lanes == subs, noise_row, 0.0)
        b_ref[...] = sides
        root_col = jnp.sqrt(noise_col_ref[k])
        roots = [root_col[j : j + 1, :] for j in range(obs)]
        eliminate(a_ref, b_ref, roots, mem, obs, obs)
        joined = lax.dot_general(
            a_ref[...], b_ref[...], (((0,), (0,)), ((), ())), precision=highest, preferred_element_type=f32
        )
        gain_t = joined[:, mem : mem + 1] - joined
        gain = gain_t.T[:mem, :]

        s_high, s_low = split(spread)
        stacked = jnp.concatenate([s_high.astype(f32), s_high.astype(f32), s_low.astype(f32)], axis=0)
        left = stacked.T.astype(bf16)
        g_high, g_low = split(gain)
        gains = jnp.concatenate([g_high, g_high, g_low], axis=1)

        cell_col = cell_col_ref[k]
        from_tile = cell_col // CELL_DEV
        from_within = cell_col - from_tile * CELL_DEV
        from_row = from_within // LON_DEV
        from_col = (from_tile * LON_DEV + from_within - from_row * LON_DEV).astype(f32)
        from_row = from_row.astype(f32)
        from_tile = from_tile.astype(f32)

        def renew(b, carry):
            @pl.when(2 * b + 1 > k)
            def _():
                upcoming = jnp.concatenate([probes[2 * b], probes[2 * b + 1]], axis=1)
                high, low = split(upcoming)
                crossed = dot(left, jnp.concatenate([high, low, high], axis=0))
                weights = []
                for u in range(2):
                    weight = tapered_weight(
                        from_row, from_col, target_row_ref_get(b, u), target_col_ref_get(b, u), circle
                    )
                    apart = jnp.abs(from_tile - target_tile_ref_get(b, u))
                    near = (apart < 1.5) | (apart > axis_size - 1.5)
                    weights.append(jnp.where(near, weight * scale, 0.0))
                tapered = crossed * jnp.concatenate(weights, axis=1)
                high, low = split(tapered)
                upcoming = upcoming + dot(gains, jnp.concatenate([high, low, high], axis=0))
                probes[2 * b] = upcoming[:, :obs]
                probes[2 * b + 1] = upcoming[:, obs:]

            return carry

        def target_row_ref_get(b, u):
            return target_row[2 * b + u]

        def target_col_ref_get(b, u):
            return target_col[2 * b + u]

        def target_tile_ref_get(b, u):
            return target_tile[2 * b + u]

        for b in range(batches // 2):
            renew(b, 0)

        listed = list_ref[k]
        chosen = lanes[:slots] == listed
        select = chosen.astype(bf16)
        pick_row = cell_row_ref[k]
        pick_tile = pick_row // CELL_DEV
        pick_within = pick_row - pick_tile * CELL_DEV
        pick_r = pick_within // LON_DEV
        pick_c = (pick_tile * LON_DEV + pick_within - pick_r * LON_DEV).astype(f32)
        list_row = jnp.sum(jnp.where(chosen, pick_r.astype(f32), 0.0), axis=1, keepdims=True)
        list_col = jnp.sum(jnp.where(chosen, pick_c, 0.0), axis=1, keepdims=True)
        usable = jnp.where(listed < obs, scale, 0.0)
        weight = tapered_weight(list_row, list_col, here_row, here_col, circle) * usable
        left_listed = dot(select, left).astype(bf16)
        gt_high, gt_low = split(gain_t)
        gt_high = dot(select, gt_high)
        gt_low = dot(select, gt_low)
        gains_listed = jnp.concatenate([gt_high, gt_high, gt_low, jnp.zeros((obs - 3 * slots, obs), f32)], axis=0)
        gains_listed = gains_listed.T[:mem, : 3 * slots].astype(bf16)

        def spread_level(level, carry, source):
            block = source[level]
            high, low = split(block)
            crossed = dot(left_listed, jnp.concatenate([high, low, high], axis=0))
            high, low = split(crossed * weight)
            out_ref[level] = block + dot(gains_listed, jnp.concatenate([high, low, high], axis=0))
            return carry

        lax.fori_loop(0, levels, functools.partial(spread_level, source=out_ref), 0)
        return carry

    out_ref[...] = x_ref[...]
    lax.fori_loop(0, batches, turn, 0)


def body(ensemble, obs_cell, obs_value, obs_noise, obs_weight, tile_lists, batch_order):
    mem, levels, cells = ensemble.shape
    batches = obs_cell.shape[0]
    axis_size = lax.axis_size("lon")
    obs = obs_cell.shape[1] * axis_size
    slots = 32
    cell_table = lax.all_gather(obs_cell, "lon", axis=1, tiled=True)
    observed = lax.all_gather(obs_value, "lon", axis=1, tiled=True)
    noise = lax.all_gather(obs_noise, "lon", axis=1, tiled=True)
    offset = lax.axis_index("lon") * CELL_DEV

    cell_table = cell_table[batch_order]
    observed = observed[batch_order]
    noise = noise[batch_order]
    weights = obs_weight[batch_order]
    lists = tile_lists[batch_order]

    owned = ((cell_table >= offset) & (cell_table < offset + CELL_DEV)).astype(f32)
    within = jnp.clip(cell_table - offset, 0, CELL_DEV - 1)

    def portion_of(inside, mine, weight):
        picked = jnp.take(ensemble, inside, axis=2)
        return jnp.sum(picked * (weight * mine[None, :])[None], axis=1)

    probes = lax.psum(jax.vmap(portion_of)(within, owned, weights), ("lon", "lev"))
    lists = jnp.pad(lists, ((0, 0), (0, slots - lists.shape[1])), constant_values=obs)

    call = pl.pallas_call(
        functools.partial(
            kernel_body, batches=batches, levels=levels, mem=mem, obs=obs, cells=cells, slots=slots,
            axis_size=axis_size,
        ),
        out_shape=jax.ShapeDtypeStruct((levels, mem, cells), f32),
        in_specs=[pl.BlockSpec(memory_space=pltpu.VMEM)] * 8,
        out_specs=pl.BlockSpec(memory_space=pltpu.VMEM),
        scratch_shapes=[
            pltpu.VMEM((batches, mem, obs), f32),
            pltpu.VMEM((obs, obs), f32),
            pltpu.VMEM((obs, obs), f32),
        ],
        compiler_params=pltpu.CompilerParams(vmem_limit_bytes=40 * 1024 * 1024),
        name="assimilate",
    )
    out = call(
        ensemble.transpose(1, 0, 2),
        probes,
        observed[:, None, :],
        noise[:, None, :],
        noise[:, :, None],
        cell_table[:, None, :],
        cell_table[:, :, None],
        lists[:, :, None],
    )
    return out.transpose(1, 0, 2)


def solution(mesh):
    return jax.shard_map(
        body,
        mesh=mesh,
        in_specs=(
            P(None, "lev", "lon"),
            P(None, "lon"),
            P(None, "lon"),
            P(None, "lon"),
            P(None, "lev", None),
            P(None, "lon"),
            P(),
        ),
        out_specs=P(None, "lev", "lon"),
        check_vma=False,
    )
```

time: 1300 us -> 350 us (0.27)
  other arithmetic: 560 us -> 6.22 us
  matrix products: 301 us -> 0 us
  local copies, waits for them, and re-layouts: 219 us -> 27.4 us
  Pallas kernels: 0 us -> 143 us
  blocking collectives: 119 us -> 88.6 us
  loops' own time: 28.4 us -> 0 us
  waiting for transfers between devices: 44.6 us -> 67.6 us
    another operation x72 -> x0, other arithmetic: 401 us -> none  [the longest x36 150 us: gain_parts(): factor = jnp.linalg.cholesky(covariance)]
    dot_general x108 -> x0, matrix products: 284 us -> none  [the longest x12 76.3 us: update_block(): jnp.dot(spread[:, chosen].T, flattened, precision=highest) / (MEM - 1)]
    pallas_call x0 -> x1, Pallas kernels: none -> 143 us  [body(): call(ensemble.transpose(1, 0, 2), probes, observed[:, None, :], noise[:,...]
    reduce_or x18 -> x0, other arithmetic: 123 us -> none  [the longest x12 122 us: correct(): member = jnp.any(lists_rows[:, :, None] == numbers[None, None, :], axis=1)]
    gather x63 -> x8, local copies, waits for them, and re-layouts: 98.5 us -> 9.83 us  [the longest x1 6.68 us: portion_of(): picked = jnp.take(ensemble, inside, axis=2)]
    while x342 -> x0, local copies, waits for them, and re-layouts: 83.3 us -> none
    all_gather x3 -> x2, blocking collectives: 91.5 us -> 61 us  [the longest x1 31.3 us: body(): noise = lax.all_gather(obs_noise, 'lon', axis=1, tiled=True)]
    another operation x1 -> x0, loops' own time: 28.4 us -> none  [body(): finished = lax.fori_loop(0, BATCHES // 4, grouped, carried)]
  transfers between devices with their start and end apart: 1 -> 1, of which waited for: 1 -> 1; matrix products, arithmetic and copies ran while one was open for 0% -> 2% of each run, Pallas kernels for 0% -> 0%
where the time goes in v1:
time: 350 us; the launch traced here: 346 us
  Pallas kernels  143 us (41%)
  blocking collectives  88.6 us (25%)
  waiting for transfers between devices  67.6 us (19%)
  local copies, waits for them, and re-layouts  27.4 us (8%)
  between operations  13.5 us (4%)
  other arithmetic  6.22 us (2%)
    pallas_call x1, Pallas kernels, body(): call(ensemble.transpose(1, 0, 2), probes, observed[:, None, :], noise[:,...  143 us
    psum x1, waiting for transfers between devices, body(): lax.psum(jax.vmap(portion_of)(within, owned, weights), ('lon', 'lev'))  67.6 us
    all_gather x1, blocking collectives, body(): noise = lax.all_gather(obs_noise, 'lon', axis=1, tiled=True)  31.3 us
    all_gather x1, blocking collectives, body(): observed = lax.all_gather(obs_value, 'lon', axis=1, tiled=True)  29.7 us
    all_gather x1, blocking collectives, body(): cell_table = lax.all_gather(obs_cell, 'lon', axis=1, tiled=True)  27.6 us
    unnamed x14, local copies, waits for them, and re-layouts  11.1 us
  transfers between devices with their start and end apart: 1, of which 1 were waited for; matrix products, arithmetic and copies ran while one was open for 2% of the time, Pallas kernels for 0%

profile of v1, /device:TPU:29, one launch (start us, length us, event | category | flops | bytes accessed | tf_op | source)
XLA Modules:
  0.0 346.3 jit_solution(1357212882481267182)
XLA Ops:
  6.5 0.0 copy-start
  6.5 0.0 all-reduce.3.cloned.1.call-start
  6.5 0.7 compare_select_fusion.2
  7.2 27.6 %all_gather.9 = s32[12,128]{0,1:T(8,128)S(1)} all-gather(s32[12,8]{0,1:T(8,128)} %param.8), channel_id=1, replica_groups=mesh['lon'=16,'lev'=2] {'lon'}, dimensions={1}, use_global_device_ids=true | all-gather | bytes 6528 | tf_op jit(solution)/shard_map/all_gather | solution.py:220
  34.8 0.1 copy.24
  34.9 0.6 gather_fusion
  35.5 0.0 copy-done
  35.5 0.6 gather_fusion.2
  36.1 0.3 copy.26
  36.4 4.7 %copy.25 = f32[80,8,1024]{0,1,2:T(8,128)} copy(f32[80,8,1024]{2,1,0:T(8,128)} %param.7) | data formatting | bytes 5242880 | tf_op args[0]
  41.1 6.7 %gather_fusion.1 = f32[1536,80,8]{1,2,0:T(8,128)} fusion(f32[80,8,1024]{0,1,2:T(8,128)} %copy.25, s32[2048]{0:T(1024)S(1)} %pad_clamp_fusion), kind=kCustom, calls=%fused_computation.1 | custom fusion | bytes 7870464 | tf_op jit(solution)/shard_map/vmap(jit(_take))/gather | solution.py:235
  47.8 0.0 copy-start.5
  47.8 5.5 %fusion = f32[12,80,128]{1,2,0:T(8,128)S(1)} fusion(f32[12,128,80,8]{2,3,1,0:T(8,128)} %bitcast.18, f32[12,8,128]{1,2,0:T(8,128)S(1)} %copy.26, pred[12,128]{1,0:T(8,128)(4,1)S(1)} %get-tuple-element.5), kind=kLoop, calls=%fused_computation.7 | loop fusion | flops 2826240 | bytes 4474368 | tf_op jit(solution)/shard_map/vmap()/reduce_sum | solution.py:236
  53.3 0.0 copy-start.4
  53.3 1.0 copy.27
  54.4 0.0 all-reduce.3.cloned.1.call-update
  54.4 3.3 copy.35
  57.7 0.3 copy.31.cell_col_ref
  58.0 0.0 copy-done.5
  58.0 31.3 %all_gather.11 = f32[12,128]{0,1:T(8,128)S(1)} all-gather(f32[12,8]{0,1:T(8,128)S(1)} %copy-done.5), channel_id=1, replica_groups=mesh['lon'=16,'lev'=2] {'lon'}, dimensions={1}, use_global_device_ids=true | all-gather | bytes 6528 | tf_op jit(solution)/shard_map/all_gather | solution.py:222
  89.2 0.1 copy.29
  89.3 0.6 gather_fusion.4
  89.9 1.2 copy.30.noise_col_ref
  91.1 0.0 copy-done.4
  91.1 0.6 gather_fusion.5
  91.6 0.8 copy.32.list_ref
  92.5 29.7 %all_gather.10 = f32[12,128]{0,1:T(8,128)S(1)} all-gather(f32[12,8]{0,1:T(8,128)} %param.9), channel_id=1, replica_groups=mesh['lon'=16,'lev'=2] {'lon'}, dimensions={1}, use_global_device_ids=true | all-gather | bytes 6528 | tf_op jit(solution)/shard_map/all_gather | solution.py:221
  122.2 0.1 copy.28
  122.3 0.6 gather_fusion.3
  122.9 67.6 %all-reduce.3.cloned.1.call-done.probe_ref = f32[12,80,128]{2,1,0:T(8,128)} async-done(((f32[12,80,128]{2,1,0:T(8,128)}), f32[12,80,128]{2,1,0:T(8,128)}) %all-reduce.3.cloned.1.call-update) | async-done | bytes 491536 | tf_op jit(solution)/shard_map/psum | solution.py:238
  190.4 0.0 copy-start.1
  190.4 1.1 copy-done.1
  191.5 0.0 copy-start.2
  191.5 0.9 copy-done.2
  192.5 0.0 copy-start.3
  192.5 1.0 copy-done.3
  193.5 142.9 %assimilate.1 = f32[8,80,1024]{2,1,0:T(8,128)S(1)} custom-call(f32[8,80,1024]{2,1,0:T(8,128)S(1)} %bitcast.16, f32[12,80,128]{2,1,0:T(8,128)S(1)} %copy-done.3, f32[12,1,128]{2,1,0:T(1,128)S(1)} %broadcast_in_dim.36.value_ref, f32[12,1,128]{2,1,0:T(1,128)S(1)} %broadcast_in_dim.37.noise_ref, f32[12,128,1]{2,1,0:T(8,128)S(1)} %copy-done.1, ...), custom_call_target="tpu_custom_call" | custom-call | tf_op jit(solution)/shard_map/assimilate/pallas_call | solution.py:257
  336.4 3.0 copy.33
  (9 shorter events, 0.1 us)
Async XLA Ops:
  6.5 29.0 %copy-start = (f32[12,8,128]{2,1,0:T(8,128)S(1)}, f32[12,8,128]{2,1,0:T(8,128)}, u32[]{:S(2)}) copy-start(f32[12,8,128]{2,1,0:T(8,128)} %param.11) | copy-start | bytes 147460
  6.5 183.9 %all-reduce.3.cloned.1.call-start = ((), (), s32[]{:S(2)}) async-start(), calls=%async_computation | async-start | bytes 983040 | tf_op jit(solution)/shard_map/psum | solution.py:238
  47.8 10.2 %copy-start.5 = (f32[12,8]{0,1:T(8,128)S(1)}, f32[12,8]{0,1:T(8,128)}, u32[]{:S(2)}) copy-start(f32[12,8]{0,1:T(8,128)} %param.10) | copy-start | bytes 1156
  53.3 37.8 %copy-start.4 = (s32[12,24]{1,0:T(8,128)S(1)}, s32[12,24]{1,0:T(8,128)}, u32[]{:S(2)}) copy-start(s32[12,24]{1,0:T(8,128)} %param.12) | copy-start | bytes 3460
  190.4 1.1 copy-start.1
  191.5 0.9 copy-start.2
  192.5 1.0 copy-start.3
Sparse Core Ops, SparseCore 0:
  54.5 135.8 all-reduce.2

commit v2 on v1

--- a/solution.py
+++ b/solution.py
@@ -211,15 +211,155 @@
     lax.fori_loop(0, batches, turn, 0)
 
 
+def peer_of(d, ranks, both):
+    lon, lev = lax.axis_index("lon"), lax.axis_index("lev")
+    if not both:
+        return lax.rem(lon + d, ranks), lev
+    cores = lax.axis_size("lev")
+    number = lax.rem(lon * cores + lev + d, ranks)
+    return lax.div(number, cores), lax.rem(number, cores)
+
+
+def meet(ranks, both):
+    barrier = pltpu.get_barrier_semaphore()
+
+    def announce(d, carry):
+        pl.semaphore_signal(
+            barrier, inc=1, device_id=peer_of(d, ranks, both), device_id_type=pl.DeviceIdType.MESH
+        )
+        return carry
+
+    lax.fori_loop(1, ranks, announce, 0)
+    pl.semaphore_wait(barrier, ranks - 1)
+
+
+def each_peer(ranks, copy_to):
+    def start(d, carry):
+        copy_to(d).start()
+        return carry
+
+    def finish(d, carry):
+        copy_to(d).wait()
+        return carry
+
+    return (
+        lambda: lax.fori_loop(1, ranks, start, 0),
+        lambda: lax.fori_loop(1, ranks, finish, 0),
+    )
+
+
+def table_kernel(mine_ref, out_ref, landed, send_sem, recv_sem, *, ranks):
+    meet(ranks, False)
+
+    def copy_to(d):
+        return pltpu.make_async_remote_copy(
+            src_ref=mine_ref,
+            dst_ref=landed.at[d],
+            send_sem=send_sem.at[d],
+            recv_sem=recv_sem.at[d],
+            device_id=peer_of(d, ranks, False),
+            device_id_type=pl.DeviceIdType.MESH,
+        )
+
+    start, finish = each_peer(ranks, copy_to)
+    start()
+    landed[0] = mine_ref[...]
+    finish()
+    out_ref[...] = jnp.sum(landed[...], axis=0)
+
+
+def sum_kernel(mine_ref, out_ref, landed, total, send_sem, recv_sem, send_again, recv_again, *, ranks, rows):
+    meet(ranks, True)
+    me = lax.axis_index("lon") * lax.axis_size("lev") + lax.axis_index("lev")
+    own = pl.ds(pl.multiple_of(me * rows, rows), rows)
+
+    def scatter_to(d):
+        other = lax.rem(me + d, ranks)
+        return pltpu.make_async_remote_copy(
+            src_ref=mine_ref.at[pl.ds(pl.multiple_of(other * rows, rows), rows)],
+            dst_ref=landed.at[d],
+            send_sem=send_sem.at[d],
+            recv_sem=recv_sem.at[d],
+            device_id=peer_of(d, ranks, True),
+            device_id_type=pl.DeviceIdType.MESH,
+        )
+
+    def gather_to(d):
+        return pltpu.make_async_remote_copy(
+            src_ref=total,
+            dst_ref=out_ref.at[own],
+            send_sem=send_again.at[d],
+            recv_sem=recv_again.at[d],
+            device_id=peer_of(d, ranks, True),
+            device_id_type=pl.DeviceIdType.MESH,
+        )
+
+    start, finish = each_peer(ranks, scatter_to)
+    start()
+    landed[0] = mine_ref[own]
+    finish()
+    total[...] = jnp.sum(landed[...], axis=0)
+    start, finish = each_peer(ranks, gather_to)
+    start()
+    out_ref[own] = total[...]
+    finish()
+
+
+def gathered_table(parts, axis_size):
+    rows, own = parts.shape
+    padded = -(-rows // 8) * 8
+    width = own * axis_size
+    lane = jnp.arange(width, dtype=jnp.int32)[None, :]
+    placed = jnp.where(lane // own == lax.axis_index("lon"), jnp.tile(parts, (1, axis_size)), 0.0)
+    placed = jnp.pad(placed, ((0, padded - rows), (0, 0)))
+    return pl.pallas_call(
+        functools.partial(table_kernel, ranks=axis_size),
+        out_shape=jax.ShapeDtypeStruct((padded, width), f32),
+        in_specs=[pl.BlockSpec(memory_space=pltpu.VMEM)],
+        out_specs=pl.BlockSpec(memory_space=pltpu.VMEM),
+        scratch_shapes=[
+            pltpu.VMEM((axis_size, padded, width), f32),
+            pltpu.SemaphoreType.DMA((axis_size,)),
+            pltpu.SemaphoreType.DMA((axis_size,)),
+        ],
+        compiler_params=pltpu.CompilerParams(collective_id=0, has_side_effects=True),
+        name="table",
+    )(placed)[:rows]
+
+
+def summed(portions, ranks):
+    count, width = portions.shape
+    rows = -(-count // (8 * ranks)) * 8
+    padded = jnp.pad(portions, ((0, rows * ranks - count), (0, 0)))
+    return pl.pallas_call(
+        functools.partial(sum_kernel, ranks=ranks, rows=rows),
+        out_shape=jax.ShapeDtypeStruct(padded.shape, f32),
+        in_specs=[pl.BlockSpec(memory_space=pltpu.VMEM)],
+        out_specs=pl.BlockSpec(memory_space=pltpu.VMEM),
+        scratch_shapes=[
+            pltpu.VMEM((ranks, rows, width), f32),
+            pltpu.VMEM((rows, width), f32),
+            pltpu.SemaphoreType.DMA((ranks,)),
+            pltpu.SemaphoreType.DMA((ranks,)),
+            pltpu.SemaphoreType.DMA((ranks,)),
+            pltpu.SemaphoreType.DMA((ranks,)),
+        ],
+        compiler_params=pltpu.CompilerParams(collective_id=1, has_side_effects=True),
+        name="total",
+    )(padded)[:count]
+
+
 def body(ensemble, obs_cell, obs_value, obs_noise, obs_weight, tile_lists, batch_order):
     mem, levels, cells = ensemble.shape
     batches = obs_cell.shape[0]
     axis_size = lax.axis_size("lon")
     obs = obs_cell.shape[1] * axis_size
     slots = 32
-    cell_table = lax.all_gather(obs_cell, "lon", axis=1, tiled=True)
-    observed = lax.all_gather(obs_value, "lon", axis=1, tiled=True)
-    noise = lax.all_gather(obs_noise, "lon", axis=1, tiled=True)
+    parts = jnp.concatenate([obs_cell.astype(f32), obs_value, obs_noise], axis=0)
+    table = gathered_table(parts, axis_size)
+    cell_table = table[:batches].astype(jnp.int32)
+    observed = table[batches : 2 * batches]
+    noise = table[2 * batches :]
     offset = lax.axis_index("lon") * CELL_DEV
 
     cell_table = cell_table[batch_order]
@@ -235,7 +375,8 @@
         picked = jnp.take(ensemble, inside, axis=2)
         return jnp.sum(picked * (weight * mine[None, :])[None], axis=1)
 
-    probes = lax.psum(jax.vmap(portion_of)(within, owned, weights), ("lon", "lev"))
+    portions = jax.vmap(portion_of)(within, owned, weights).reshape(batches * mem, obs)
+    probes = summed(portions, axis_size * lax.axis_size("lev")).reshape(batches, mem, obs)
     lists = jnp.pad(lists, ((0, 0), (0, slots - lists.shape[1])), constant_values=obs)
 
     call = pl.pallas_call(

time: 350 us -> 224 us (0.64)
  blocking collectives: 88.6 us -> 0 us
  waiting for transfers between devices: 67.6 us -> 0 us
  Pallas kernels: 143 us -> 190 us
  between operations: 13.5 us -> 0.19 us
    all_gather x3 -> x0, blocking collectives: 88.6 us -> none  [the longest x1 31.3 us: body(): noise = lax.all_gather(obs_noise, 'lon', axis=1, tiled=True)]
    psum x1 -> x0, waiting for transfers between devices: 67.6 us -> none  [body(): lax.psum(jax.vmap(portion_of)(within, owned, weights), ('lon', 'lev'))]
    pallas_call x0 -> x2, Pallas kernels: none -> 47.3 us  [the longest x1 36 us: summed(): pl.pallas_call(functools.partial(sum_kernel, ranks=ranks, rows=rows), out...]
    unnamed x14 -> x6, local copies, waits for them, and re-layouts: 11.1 us -> 8 us
  transfers between devices with their start and end apart: 1 -> 0, of which waited for: 1 -> 0; matrix products, arithmetic and copies ran while one was open for 2% -> 0% of each run, Pallas kernels for 0% -> 0%
where the time goes in v2:
time: 224 us; the launch traced here: 223 us
  Pallas kernels  190 us (85%)
  local copies, waits for them, and re-layouts  24.4 us (11%)
  other arithmetic  8.42 us (4%)
    pallas_call x1, Pallas kernels, body(): call(ensemble.transpose(1, 0, 2), probes, observed[:, None, :], noise[:,...  143 us
    pallas_call x1, Pallas kernels, summed(): pl.pallas_call(functools.partial(sum_kernel, ranks=ranks, rows=rows), out...  36 us
    pallas_call x1, Pallas kernels, gathered_table(): pl.pallas_call(functools.partial(table_kernel, ranks=axis_size), out_shap...  11.4 us
    unnamed x6, local copies, waits for them, and re-layouts  8 us
    gather x1, local copies, waits for them, and re-layouts, portion_of(): picked = jnp.take(ensemble, inside, axis=2)  6.68 us
    reduce_sum x1, other arithmetic, portion_of(): return jnp.sum(picked * (weight * mine[None, :])[None], axis=1)  5.45 us

profile of v2, /device:TPU:29, one launch (start us, length us, event | category | flops | bytes accessed | tf_op | source)
XLA Modules:
  0.0 223.1 jit_solution(4745250013141297891)
XLA Ops:
  0.0 0.0 copy-start
  0.0 0.7 compare_select_fusion.2
  0.7 0.7 convert_element_type.17
  1.4 0.8 pad_maximum_fusion
  2.2 0.1 copy.20
  2.2 0.6 pad.12.mine_ref
  2.9 11.4 %table.1 = f32[40,128]{1,0:T(8,128)} custom-call(f32[40,128]{1,0:T(8,128)} %pad.12.mine_ref), custom_call_target="tpu_custom_call" | custom-call | tf_op jit(solution)/shard_map/table/pallas_call | solution.py:315
  14.3 0.8 fusion.3
  15.0 0.6 gather_fusion
  15.6 0.0 copy-done
  15.6 0.6 gather_fusion.2
  16.2 0.3 copy.22
  16.5 4.7 %copy.21 = f32[80,8,1024]{0,1,2:T(8,128)} copy(f32[80,8,1024]{2,1,0:T(8,128)} %param.7) | data formatting | bytes 5242880 | tf_op args[0]
  21.2 6.7 %gather_fusion.1 = f32[1536,80,8]{1,2,0:T(8,128)} fusion(f32[80,8,1024]{0,1,2:T(8,128)} %copy.21, s32[2048]{0:T(1024)S(1)} %pad_clamp_fusion), kind=kCustom, calls=%fused_computation.1 | custom fusion | bytes 7870464 | tf_op jit(solution)/shard_map/vmap(jit(_take))/gather | solution.py:375
  27.9 0.0 copy-start.1
  27.9 5.4 %fusion = f32[12,80,128]{1,2,0:T(8,128)S(1)} fusion(f32[12,128,80,8]{2,3,1,0:T(8,128)} %bitcast.23, f32[12,8,128]{1,2,0:T(8,128)S(1)} %copy.22, pred[12,128]{1,0:T(8,128)(4,1)S(1)} %get-tuple-element.8), kind=kLoop, calls=%fused_computation.7 | loop fusion | flops 2826240 | bytes 4474368 | tf_op jit(solution)/shard_map/vmap()/reduce_sum | solution.py:376
  33.4 0.3 copy.23
  33.6 0.8 pad.13.mine_ref
  34.5 36.0 %total.1 = f32[1024,128]{1,0:T(8,128)} custom-call(f32[1024,128]{1,0:T(8,128)} %pad.13.mine_ref), custom_call_target="tpu_custom_call" | custom-call | tf_op jit(solution)/shard_map/total/pallas_call | solution.py:334
  70.4 1.1 slice.17
  71.5 0.3 copy.25.cell_col_ref
  71.8 0.6 gather_fusion.4
  72.4 0.3 copy.24.noise_col_ref
  72.7 0.6 gather_fusion.3
  73.3 0.0 copy-done.1
  73.3 0.6 gather_fusion.5
  73.9 0.2 copy.26.list_ref
  74.0 3.3 %copy.29 = f32[80,8,1024]{2,0,1:T(8,128)S(1)} copy(f32[80,8,1024]{2,1,0:T(8,128)} %param.7) | data formatting | bytes 5242880 | tf_op args[0]
  77.3 142.8 %assimilate.1 = f32[8,80,1024]{2,1,0:T(8,128)S(1)} custom-call(f32[8,80,1024]{2,1,0:T(8,128)S(1)} %bitcast.21, f32[12,80,128]{2,1,0:T(8,128)S(1)} %bitcast.22, f32[12,1,128]{2,1,0:T(1,128)S(1)} %broadcast_in_dim.51.value_ref, f32[12,1,128]{2,1,0:T(1,128)S(1)} %broadcast_in_dim.52.noise_ref, f32[12,128,1]{2,1,0:T(8,128)S(1)} %copy.24.noise_col_ref, ...), custom_call_target="tpu_custom_call" | custom-call | tf_op jit(solution)/shard_map/assimilate/pallas_call | solution.py:398
  220.1 3.0 %copy.27 = f32[80,8,1024]{2,1,0:T(8,128)} copy(f32[80,8,1024]{2,0,1:T(8,128)S(1)} %bitcast.20) | data formatting | bytes 5242880 | tf_op jit(solution)/shard_map/transpose | solution.py:408
  (12 shorter events, 0.1 us)
Async XLA Ops:
  0.0 15.6 %copy-start = (f32[12,8,128]{2,1,0:T(8,128)S(1)}, f32[12,8,128]{2,1,0:T(8,128)}, u32[]{:S(2)}) copy-start(f32[12,8,128]{2,1,0:T(8,128)} %param.11) | copy-start | bytes 147460
  27.9 45.3 %copy-start.1 = (s32[12,24]{1,0:T(8,128)S(1)}, s32[12,24]{1,0:T(8,128)}, u32[]{:S(2)}) copy-start(s32[12,24]{1,0:T(8,128)} %param.12) | copy-start | bytes 3460
